TPU v7x, 128 devices: a whole 4x4x4 slice. The times are simulated.
128 devices in a mesh: row: 16 (over z_hi, y, core), col: 8 (over z_lo, x).
Axes of the slice: x: 4, y: 4, z: 4 (z_hi: 2, z_lo: 2; z = z_hi * 2 + z_lo), core: 2. Of those that a mesh axis runs over, the one named last changes fastest.
Arguments:
- parent_inverse: float32 [24576, 24576], P('row', 'col'), may hold values from -6 to 6
- panel: float32 [24576, 1024], P(('col', 'row')), may hold values from -0.0390625 to 0.0390625
- saved_diag: float32 [1024, 1024], P('row', 'col'), may hold values from -6 to 6
Outputs:
- offdiag_block: float32 [24576, 1024], P(('row', 'col'))
- diag_block: float32 [1024, 1024], P('row', 'col')
All inputs are finite; a program needn't handle non-finite values.
Results may differ from a plain program's by a relative error of at most 0.00007.
Values sent between devices are 32-bit elements; how exact they have to be, the bound alone decides.
A program may use at most 128 MiB of HBM per device.

v0:
```python
import jax
import jax.numpy as jnp
from jax import lax
from jax.sharding import PartitionSpec as P


def spread(block, axis, holder):
    block = jnp.where(lax.axis_index(axis) == holder, block, jnp.zeros_like(block))
    return lax.psum(block, axis)


def shards(parent_inverse, panel, saved_diag):
    block_rows = parent_inverse.shape[0]
    column_count = lax.axis_size("col")
    keep_rows = block_rows // column_count
    column_panel = lax.all_gather(panel, "row", axis=0, tiled=True)
    row_index = lax.axis_index("row")
    column_index = lax.axis_index("col")
    local_half = lax.dynamic_slice_in_dim(column_panel, row_index % 2 * block_rows, block_rows, 0)
    product = lax.psum_scatter(
        jnp.dot(
            parent_inverse,
            column_panel,
            precision=lax.Precision.HIGHEST,
            preferred_element_type=jnp.float32,
        ),
        "col",
        scatter_dimension=0,
        tiled=True,
    )
    panel_half = spread(local_half, "col", row_index // 2)
    own_rows = lax.dynamic_slice_in_dim(panel_half, column_index * keep_rows, keep_rows, 0)
    offdiag_block = -product
    partial_value = lax.dot_general(
        own_rows,
        product,
        (((0,), (0,)), ((), ())),
        precision=lax.Precision.HIGHEST,
        preferred_element_type=jnp.float32,
    )
    by_columns = lax.psum_scatter(partial_value, "col", scatter_dimension=1, tiled=True)
    summed = lax.psum_scatter(by_columns, "row", scatter_dimension=0, tiled=True)
    diag_block = saved_diag + summed
    return (offdiag_block, diag_block)


def solution(mesh):
    in_specs = (P("row", "col"), P(("col", "row"), None), P("row", "col"))
    out_specs = (P(("row", "col"), None), P("row", "col"))
    return jax.shard_map(shards, mesh=mesh, in_specs=in_specs, out_specs=out_specs, check_vma=False)
```

profile of v0, /device:TPU:96, one launch (start us, length us, event | category | flops | bytes accessed | tf_op | source)
XLA Modules:
  0.0 460.1 jit_solution(5138972015593387433)
XLA Ops:
  7.2 0.0 all-gather.2.cloned.1.call-start
  7.2 0.7 all-gather.2.cloned.1.call-update
  7.9 0.0 all-reduce.2.cloned.1.call-start
  8.0 92.4 %all-gather.2.cloned.1.call-done = f32[3072,1024]{1,0:T(8,128)} async-done(((f32[192,1024]{1,0:T(8,128)}), f32[3072,1024]{1,0:T(8,128)}) %all-gather.2.cloned.1.call-update) | async-done | bytes 12582928 | tf_op jit(solution)/shard_map/all_gather | solution.py:16
  100.4 6.8 %dynamic-slice_select_fusion = f32[1536,1024]{1,0:T(8,128)} fusion(f32[3072,1024]{1,0:T(8,128)} %all-gather.2.cloned.1.call-done, s32[]{:T(128)S(6)} %select_n.28, pred[]{:T(512)S(6)} %eq.5), kind=kLoop, calls=%fused_computation | loop fusion | flops 1572864 | bytes 12582917 | tf_op jit(solution)/shard_map/jit(_where)/select_n | solution.py:8
  107.1 0.0 all-reduce.2.cloned.1.call-update
  107.2 0.0 reduce-scatter.4.cloned.1.call-start
  107.2 66.9 %fusion.3 = f32[1536,1024]{1,0:T(8,128)} fusion(f32[1536,3072]{1,0:T(8,128)} %param.3, f32[3072,1024]{1,0:T(8,128)} %all-gather.2.cloned.1.call-done), kind=kOutput, calls=%fused_computation.4 | convolution fusion | flops 57982058496 | bytes 37748736 | tf_op jit(solution)/shard_map/dot_general | solution.py:21
  174.1 0.0 reduce-scatter.4.cloned.1.call-update
  174.1 0.0 copy-start.1
  174.2 0.2 reduce-scatter.6.cloned.1.call-start
  174.4 76.3 %all-reduce.2.cloned.1.call-done = f32[1536,1024]{1,0:T(8,128)} async-done(((f32[1536,1024]{1,0:T(8,128)}), f32[1536,1024]{1,0:T(8,128)}) %all-reduce.2.cloned.1.call-update) | async-done | bytes 6291472 | tf_op jit(solution)/shard_map/psum | solution.py:9
  250.7 74.2 %reduce-scatter.4.cloned.1.call-done = f32[192,1024]{1,0:T(8,128)} async-done(((f32[1536,1024]{1,0:T(8,128)}), f32[192,1024]{1,0:T(8,128)}) %reduce-scatter.4.cloned.1.call-update) | async-done | bytes 786448 | tf_op jit(solution)/shard_map/reduce_scatter | solution.py:20
  325.0 0.0 copy-start
  325.0 6.9 %fusion = f32[1024,1024]{1,0:T(8,128)} fusion(f32[192,1024]{1,0:T(8,128)} %reduce-scatter.4.cloned.1.call-done, f32[1536,1024]{1,0:T(8,128)} %all-reduce.2.cloned.1.call-done, s32[]{:T(128)S(6)} %select_n.30), kind=kOutput, calls=%fused_computation.1 | convolution fusion | flops 2415919104 | bytes 5767172 | tf_op jit(solution)/shard_map/dot_general | solution.py:34
  331.8 0.0 reduce-scatter.6.cloned.1.call-update
  331.8 0.0 reduce-scatter.8.cloned.1.call-start
  331.9 52.0 %reduce-scatter.6.cloned.1.call-done = f32[1024,128]{1,0:T(8,128)} async-done(((f32[1024,1024]{1,0:T(8,128)}), f32[1024,128]{1,0:T(8,128)}) %reduce-scatter.6.cloned.1.call-update) | async-done | bytes 524304 | tf_op jit(solution)/shard_map/reduce_scatter | solution.py:41
  383.9 0.0 reduce-scatter.8.cloned.1.call-update
  383.9 0.0 copy-done
  383.9 0.9 neg.3
  384.8 67.3 %reduce-scatter.8.cloned.1.call-done = f32[64,128]{1,0:T(8,128)} async-done(((f32[1024,128]{1,0:T(8,128)}), f32[64,128]{1,0:T(8,128)}) %reduce-scatter.8.cloned.1.call-update) | async-done | bytes 32784 | tf_op jit(solution)/shard_map/reduce_scatter | solution.py:42
  452.1 0.0 copy-done.1
  452.1 1.4 add.25
Async XLA Ops:
  7.2 93.2 %all-gather.2.cloned.1.call-start = ((), (), s32[]{:S(2)}) async-start(), calls=%async_computation.3 | async-start | bytes 13369344 | tf_op jit(solution)/shard_map/all_gather | solution.py:16
  7.9 242.8 %all-reduce.2.cloned.1.call-start = ((), (), s32[]{:S(2)}) async-start(), calls=%async_computation.5 | async-start | bytes 12582912 | tf_op jit(solution)/shard_map/psum | solution.py:9
  107.2 217.8 %reduce-scatter.4.cloned.1.call-start = ((), (), s32[]{:S(2)}) async-start(), calls=%async_computation.4 | async-start | bytes 7077888 | tf_op jit(solution)/shard_map/reduce_scatter | solution.py:20
  174.1 278.0 %copy-start.1 = (f32[64,128]{1,0:T(8,128)S(1)}, f32[64,128]{1,0:T(8,128)}, u32[]{:S(2)}) copy-start(f32[64,128]{1,0:T(8,128)} %param.5) | copy-start | bytes 98308
  174.2 209.7 %reduce-scatter.6.cloned.1.call-start = ((), (), s32[]{:S(2)}) async-start(), calls=%async_computation.6 | async-start | bytes 4718592 | tf_op jit(solution)/shard_map/reduce_scatter | solution.py:41
  325.0 58.9 %copy-start = (f32[192,1024]{1,0:T(8,128)S(1)}, f32[192,1024]{1,0:T(8,128)}, u32[]{:S(2)}) copy-start(f32[192,1024]{1,0:T(8,128)} %reduce-scatter.4.cloned.1.call-done) | copy-start | bytes 2359300
  331.8 120.3 %reduce-scatter.8.cloned.1.call-start = ((), (), s32[]{:S(2)}) async-start(), calls=%async_computation.7 | async-start | bytes 557056 | tf_op jit(solution)/shard_map/reduce_scatter | solution.py:42
Sparse Core Ops, SparseCore 0:
  10.4 89.9 all-gather.1
  107.3 143.3 all-reduce.1
  253.1 71.7 reduce-scatter.3
  332.0 51.8 reduce-scatter.5
  387.5 64.6 reduce-scatter.7
where the time goes:
time: 462 us; the launch traced here: 460 us
  waiting for transfers between devices  363 us (79%)
  matrix products  73.8 us (16%)
  between operations  13.8 us (3%)
  other arithmetic  9.07 us (2%)
    all_gather x1, waiting for transfers between devices, shards(): column_panel = lax.all_gather(panel, 'row', axis=0, tiled=True)  92.4 us
    psum x1, waiting for transfers between devices, spread(): return lax.psum(block, axis)  76.3 us
    reduce_scatter x1, waiting for transfers between devices, shards(): lax.psum_scatter(jnp.dot(parent_inverse, column_panel, precision=lax.Prec...  74.2 us
    reduce_scatter x1, waiting for transfers between devices, shards(): lax.psum_scatter(by_columns, 'row', scatter_dimension=0, tiled=True)  67.3 us
    dot_general x1, matrix products, shards(): jnp.dot(parent_inverse, column_panel, precision=lax.Precision.HIGHEST, pr...  66.9 us
    reduce_scatter x1, waiting for transfers between devices, shards(): lax.psum_scatter(partial_value, 'col', scatter_dimension=1, tiled=True)  52 us
  transfers between devices with their start and end apart: 5, of which 5 were waited for; matrix products, arithmetic and copies ran while one was open for 15% of the time, Pallas kernels for 0%

commit v1 on v0

v1 whole, which is shorter than its diff:
```python
import jax
import jax.numpy as jnp
from jax import lax
from jax.experimental import pallas as pl
from jax.experimental.pallas import tpu as pltpu
from jax.sharding import PartitionSpec as P

MESH = pl.DeviceIdType.MESH
F32 = jnp.float32
BF16 = jnp.bfloat16
J = 4
W = 256
H = 128
R = 192
K = 3072
SLABS = K // W


def dot(a, b):
    return jnp.dot(a, b, preferred_element_type=F32)


def split(value):
    high = value.astype(BF16)
    return high, (value - high.astype(F32)).astype(BF16)


def kernel(
    pi, panel, saved, out, diag,
    pih, pil, gath, bh, bl, relay, x1r, x2f, x2b, zrec, part, rows, pth, ptl, gp, gsr, a2a, fin, fsend,
    pisem, locsem, ag_s, ag_r, rs_s, rs_r, g_s, g_r, a_s, a_r, f_s, f_r, p_s, p_r,
):
    r, c = lax.axis_index("row"), lax.axis_index("col")
    zh, y, k = r // 8, (r // 2) % 4, r % 2
    zl, x = c // 4, c % 4
    z = zh * 2 + zl
    d = 1 - 2 * k

    def dev(z_, y_, x_, k_):
        return ((z_ // 2) * 8 + y_ * 2 + k_, (z_ % 2) * 4 + x_)

    def slot(zh_, y_, k_):
        return zh_ * 8 + y_ * 2 + k_

    yf, yb, y2 = (y + d + 4) % 4, (y - d + 4) % 4, (y + 2) % 4
    zf, zb = (z + d + 4) % 4, (z - d + 4) % 4
    xf, xb, x2 = (x + d + 4) % 4, (x - d + 4) % 4, (x + 2) % 4
    zp = zh * 2 + (1 - zl)
    zo = 1 - zh
    sib = dev(z, y, x, 1 - k)
    to_yf, to_yb = dev(z, yf, x, k), dev(z, yb, x, k)
    to_zf, to_zp = dev(zf, y, x, k), dev(zp, y, x, k)
    to_xf, to_xb = dev(z, y, xf, k), dev(z, y, xb, k)
    perm_to = (2 * c + r // 8, r % 8)
    perm_block = 8 * r + c
    perm_from = (perm_block % 16, perm_block // 16)
    moves = jnp.logical_or(perm_to[0] != r, perm_to[1] != c)

    def remote(src, dst, ss, rs, to):
        return pltpu.make_async_remote_copy(
            src_ref=src, dst_ref=dst, send_sem=ss, recv_sem=rs, device_id=to, device_id_type=MESH
        )

    def own_copy(j, h):
        return pltpu.make_async_copy(
            panel.at[:, pl.ds(h * 512 + j * H, H)], gath.at[j, r, :, pl.ds(h * H, H)], locsem.at[j, h]
        )

    def slab_copy(s, b):
        return pltpu.make_async_copy(
            pi.at[:, :, pl.ds(pl.multiple_of(s * W, W), W)], part.at[b], pisem.at[b]
        )

    for j in range(J):
        for h in range(2):
            own_copy(j, h).start()
    for b in range(4):
        slab_copy(b, b).start()

    barrier = pltpu.get_barrier_semaphore()

    def greet(to):
        pl.semaphore_signal(barrier, inc=1, device_id=to, device_id_type=MESH)

    def greet_plane(i, carry):
        greet(dev((z + i // 4) % 4, (y + i % 4) % 4, x, k))
        return carry

    lax.fori_loop(1, 16, greet_plane, 0)
    greet(sib)
    for dx in range(1, 4):
        greet(dev(z, y, (x + dx) % 4, k))

    @pl.when(moves)
    def _():
        greet(perm_to)
        greet(perm_from)

    pl.semaphore_wait(barrier, jnp.where(moves, 21, 19))

    sib_slots = [slot(zh, y, k), slot(zh, yb, k), slot(zh, yf, k), slot(zo, y, k),
                 slot(zh, y2, k), slot(zo, yb, k), slot(zo, yf, k), slot(zo, y2, k)]
    from_sib = [slot(zh, y, 1 - k), slot(zh, yf, 1 - k), slot(zh, yb, 1 - k), slot(zo, y, 1 - k),
                slot(zh, y2, 1 - k), slot(zo, yf, 1 - k), slot(zo, yb, 1 - k), slot(zo, y2, 1 - k)]
    got = [slot(zh, yb, k), slot(zh, yf, k), None, slot(zo, y, k), slot(zo, yb, k), slot(zo, yf, k),
           slot(zh, y2, k), slot(zo, y2, k)]
    relay_slot = slot(zb // 2, y, k)

    def ag(j, m):
        ss, rs = ag_s.at[j, m], ag_r.at[j, m]
        if m == 2:
            return remote(gath.at[j, r], relay.at[j], ss, rs, to_zf)
        if m == 3:
            return remote(relay.at[j], gath.at[j, relay_slot], ss, rs, to_zf)
        if m >= 8:
            at = gath.at[j, sib_slots[m - 8]]
            return remote(at, at, ss, rs, sib)
        source = {0: r, 1: r, 4: got[3], 5: got[3], 6: got[0], 7: got[4]}[m]
        at = gath.at[j, source]
        return remote(at, at, ss, rs, to_yb if m in (1, 5) else to_yf)

    def ag_wait(j, m):
        if m == 2:
            at = relay.at[j]
        elif m >= 8:
            at = gath.at[j, from_sib[m - 8]]
        else:
            at = gath.at[j, got[m]]
        remote(at, at, ag_s.at[j, m], ag_r.at[j, m], sib).wait_recv()

    def p0(j):
        for h in range(2):
            own_copy(j, h).wait()
        for m in (0, 2, 1, 8):
            ag(j, m).start()

    def p1(j):
        ag_wait(j, 2)
        ag(j, 3).start()
        ag_wait(j, 0)
        ag(j, 6).start()
        ag(j, 9).start()
        ag_wait(j, 1)
        ag(j, 10).start()

    def p2(j):
        ag_wait(j, 3)
        ag(j, 4).start()
        ag(j, 5).start()
        ag(j, 11).start()
        ag_wait(j, 6)
        ag(j, 12).start()

    def p3(j):
        ag_wait(j, 4)
        ag(j, 7).start()
        ag(j, 13).start()
        ag_wait(j, 5)
        ag(j, 14).start()

    def p4(j):
        ag_wait(j, 7)
        ag(j, 15).start()

    def p5(j):
        for m in range(8, 16):
            ag_wait(j, m)

    def split_slabs(first, last):
        def body(s, carry):
            b = s % 4
            slab_copy(s, b).wait()

            def piece(q, carry):
                high, low = split(part[b, q])
                at = pl.ds(pl.multiple_of(((q % 4) * 2 + q // 4) * R, R), R)
                columns = pl.ds(pl.multiple_of(s * W, W), W)
                pih[at, columns] = high
                pil[at, columns] = low
                return carry

            lax.fori_loop(0, 8, piece, 0)

            @pl.when(s + 4 < SLABS)
            def _():
                slab_copy(s + 4, b).start()

            return carry

        lax.fori_loop(first, last, body, 0)

    def convert(j):
        def body(q, carry):
            high, low = split(gath[j, q])
            at = pl.ds(pl.multiple_of(q * R, R), R)
            bh[at, :] = high
            bl[at, :] = low
            return carry

        lax.fori_loop(0, 16, body, 0)

    def compute(j, pair):
        at = pl.ds(pl.multiple_of(pair * (2 * R), 2 * R), 2 * R)
        total = dot(pih[at, :], bh[...]) + dot(pih[at, :], bl[...]) + dot(pil[at, :], bh[...])
        part[j, pl.ds(pair * 2, 2)] = total.reshape(2, R, W)

    def rs(j, m):
        ss, rs_ = rs_s.at[j, m], rs_r.at[j, m]
        if m == 0:
            return remote(part.at[j, pl.ds(x2 * 2, 2)], x1r.at[j], ss, rs_, to_xf)
        if m == 1:
            return remote(part.at[j, pl.ds(xb * 2, 2)], x2b.at[j], ss, rs_, to_xb)
        if m == 2:
            return remote(part.at[j, pl.ds(xf * 2, 2)], x2f.at[j], ss, rs_, to_xf)
        return remote(part.at[j, x * 2 + (1 - zl)], zrec.at[j], ss, rs_, to_zp)

    def r1(j):
        rs(j, 0).wait_recv()
        at = pl.ds(xf * 2, 2)
        part[j, at] = part[j, at] + x1r[j]
        rs(j, 2).start()

    def r2(j):
        rs(j, 1).wait_recv()
        rs(j, 2).wait_recv()
        for q in (1 - zl, zl):
            part[j, x * 2 + q] = part[j, x * 2 + q] + x2f[j, q] + x2b[j, q]
        rs(j, 3).start()

    def sib_gram(j):
        return remote(gp.at[j, :, 1 - k], gsr.at[j], g_s.at[j], g_r.at[j], sib)

    def r3(j):
        rs(j, 3).wait_recv()
        product = part[j, x * 2 + zl] + zrec[j]
        out[:, j * H:(j + 1) * H] = -product[:, :H]
        out[:, 512 + j * H:512 + (j + 1) * H] = -product[:, H:]
        high, low = split(product)
        for i in range(8):
            at = pl.ds(i * H, H)
            tile = dot(pth[at, :], high) + dot(pth[at, :], low) + dot(ptl[at, :], high)
            gp[j, i] = tile.reshape(2, 64, W)
        sib_gram(j).start()

    def spread(j, i):
        z_, y_ = (z + i // 4) % 4, (y + i % 4) % 4
        source = gp.at[j, (z_ // 2) * 4 + y_, k, :, pl.ds(pl.multiple_of((z_ % 2) * H, H), H)]
        return remote(source, a2a.at[j, i], a_s.at[j, i], a_r.at[j, i], dev(z_, y_, x, k))

    def r4(j):
        sib_gram(j).wait_recv()
        for i in range(8):
            gp[j, i, k] = gp[j, i, k] + gsr[j, i]

        def body(i, carry):
            spread(j, i).start()
            return carry

        lax.fori_loop(1, 16, body, 0)

    def last(j):
        dx = (x - j + 4) % 4
        return remote(fsend.at[j], fin.at[dx], f_s.at[j], f_r.at[dx], dev(z, y, j, k))

    def r5(j):
        own = gp[j, zh * 4 + y, k, :, pl.ds(pl.multiple_of(zl * H, H), H)]

        def body(i, total):
            at = a2a.at[j, i]
            remote(at, at, a_s.at[j, i], a_r.at[j, i], sib).wait_recv()
            return total + a2a[j, i]

        total = lax.fori_loop(1, 16, body, own)
        fsend[j] = total

        @pl.when(x != j)
        def _():
            last(j).start()

    def r6(j):
        @pl.when(x == j)
        def _():
            total = saved[...] + fsend[j]
            for dx in range(1, 4):
                at = fin.at[dx]
                remote(at, at, f_s.at[j], f_r.at[dx], sib).wait_recv()
                total = total + fin[dx]
            diag[...] = total

    perm = remote(panel, rows, p_s, p_r, perm_to)
    perm_self = pltpu.make_async_copy(panel, rows, p_r)

    def perm_start():
        @pl.when(moves)
        def _():
            perm.start()

        @pl.when(jnp.logical_not(moves))
        def _():
            perm_self.start()

    def perm_take():
        @pl.when(moves)
        def _():
            perm.wait_recv()

        @pl.when(jnp.logical_not(moves))
        def _():
            perm_self.wait()

        for i in range(8):
            high, low = split(rows[:, i * H:(i + 1) * H].T)
            pth[i * H:(i + 1) * H, :] = high
            ptl[i * H:(i + 1) * H, :] = low

    p0(0)
    p0(1)
    split_slabs(0, 4)
    p1(0)
    split_slabs(4, 8)
    p2(0)
    p0(2)
    p1(1)
    split_slabs(8, 12)
    p3(0)
    p2(1)
    p4(0)
    perm_start()
    p5(0)

    services = {
        0: [lambda: (p0(3), p1(2)), lambda: p3(1), lambda: p2(2), lambda: (p4(1), p1(3), r1(0), p5(1))],
        1: [lambda: (p3(2), p2(3)), lambda: (p4(2), perm_take()), lambda: (p3(3), r2(0)), lambda: (p5(2), r1(1))],
        2: [lambda: (p4(3), r3(0)), lambda: r4(0), lambda: r2(1), lambda: (p5(3), r1(2))],
        3: [lambda: (r5(0), r3(1)), lambda: r4(1), lambda: r2(2), lambda: (r5(1), r1(3))],
    }
    for j in range(J):
        convert(j)
        compute(j, x2)
        rs(j, 0).start()
        services[j][0]()
        compute(j, xb)
        rs(j, 1).start()
        services[j][1]()
        compute(j, xf)
        services[j][2]()
        compute(j, x)
        services[j][3]()
    r3(2)
    r4(2)
    r2(3)
    r5(2)
    r3(3)
    r4(3)
    r5(3)
    for j in range(J):
        r6(j)

    for j in range(J):
        for m in range(16):
            ag(j, m).wait_send()
        for m in range(4):
            rs(j, m).wait_send()
        sib_gram(j).wait_send()

        def body(i, carry):
            spread(j, i).wait_send()
            return carry

        lax.fori_loop(1, 16, body, 0)

        @pl.when(x != j)
        def _():
            last(j).wait_send()

    @pl.when(moves)
    def _():
        perm.wait_send()


def shards(parent_inverse, panel, saved_diag):
    vmem = pl.BlockSpec(memory_space=pltpu.VMEM)
    hbm = pl.BlockSpec(memory_space=pl.ANY)
    dma = pltpu.SemaphoreType.DMA
    return pl.pallas_call(
        kernel,
        out_shape=(
            jax.ShapeDtypeStruct((R, 1024), F32),
            jax.ShapeDtypeStruct((64, H), F32),
        ),
        in_specs=[hbm, hbm, vmem],
        out_specs=(vmem, vmem),
        scratch_shapes=[
            pltpu.VMEM((8 * R, K), BF16),
            pltpu.VMEM((8 * R, K), BF16),
            pltpu.VMEM((J, 16, R, W), F32),
            pltpu.VMEM((K, W), BF16),
            pltpu.VMEM((K, W), BF16),
            pltpu.VMEM((J, R, W), F32),
            pltpu.VMEM((J, 2, R, W), F32),
            pltpu.VMEM((J, 2, R, W), F32),
            pltpu.VMEM((J, 2, R, W), F32),
            pltpu.VMEM((J, R, W), F32),
            pltpu.VMEM((J, 8, R, W), F32),
            pltpu.VMEM((R, 1024), F32),
            pltpu.VMEM((1024, R), BF16),
            pltpu.VMEM((1024, R), BF16),
            pltpu.VMEM((J, 8, 2, 64, W), F32),
            pltpu.VMEM((J, 8, 64, W), F32),
            pltpu.VMEM((J, 16, 64, H), F32),
            pltpu.VMEM((4, 64, H), F32),
            pltpu.VMEM((J, 64, H), F32),
            dma((4,)),
            dma((J, 2)),
            dma((J, 16)),
            dma((J, 16)),
            dma((J, 4)),
            dma((J, 4)),
            dma((J,)),
            dma((J,)),
            dma((J, 16)),
            dma((J, 16)),
            dma((J,)),
            dma((4,)),
            dma,
            dma,
        ],
        compiler_params=pltpu.CompilerParams(
            collective_id=0, has_side_effects=True, vmem_limit_bytes=67043328
        ),
    )(parent_inverse.reshape(8, R, K), panel, saved_diag)


def solution(mesh):
    in_specs = (P("row", "col"), P(("col", "row"), None), P("row", "col"))
    out_specs = (P(("row", "col"), None), P("row", "col"))
    return jax.shard_map(shards, mesh=mesh, in_specs=in_specs, out_specs=out_specs, check_vma=False)
```

time: 462 us -> 163 us (0.35)
  waiting for transfers between devices: 363 us -> 0 us
  Pallas kernels: 0 us -> 156 us
  matrix products: 73.8 us -> 0 us
  between operations: 13.8 us -> 0.64 us
  other arithmetic: 9.07 us -> 0 us
    reduce_scatter x3 -> x0, waiting for transfers between devices: 194 us -> none  [the longest x1 74.2 us: shards(): lax.psum_scatter(jnp.dot(parent_inverse, column_panel, precision=lax.Prec...]
    pallas_call x0 -> x1, Pallas kernels: none -> 156 us  [shards(): pl.pallas_call(kernel, out_shape=(jax.ShapeDtypeStruct((R, 1024), F32), j...]
    all_gather x1 -> x0, waiting for transfers between devices: 92.4 us -> none  [shards(): column_panel = lax.all_gather(panel, 'row', axis=0, tiled=True)]
    psum x1 -> x0, waiting for transfers between devices: 76.3 us -> none  [spread(): return lax.psum(block, axis)]
    dot_general x2 -> x0, matrix products: 73.8 us -> none  [the longest x1 66.9 us: shards(): jnp.dot(parent_inverse, column_panel, precision=lax.Precision.HIGHEST, pr...]
    select_n x1 -> x0, other arithmetic: 6.75 us -> none  [spread(): jnp.where(lax.axis_index(axis) == holder, block, jnp.zeros_like(block))]
  transfers between devices with their start and end apart: 5 -> 0, of which waited for: 5 -> 0; matrix products, arithmetic and copies ran while one was open for 15% -> 0% of each run, Pallas kernels for 0% -> 0%
where the time goes in v1:
time: 163 us; the launch traced here: 160 us
  Pallas kernels  156 us (96%)
  local copies, waits for them, and re-layouts  3.46 us (2%)
    pallas_call x1, Pallas kernels, shards(): pl.pallas_call(kernel, out_shape=(jax.ShapeDtypeStruct((R, 1024), F32), j...  156 us
    unnamed x2, local copies, waits for them, and re-layouts  3.46 us

profile of v1, /device:TPU:96, one launch (start us, length us, event | category | flops | bytes accessed | tf_op | source)
XLA Modules:
  0.0 160.3 jit_solution(11382424860516266843)
XLA Ops:
  0.6 156.2 %shard_map.50 = (f32[192,1024]{1,0:T(8,128)}, f32[64,128]{1,0:T(8,128)}) custom-call(f32[8,192,3072]{2,1,0:T(8,128)} %bitcast.1, f32[192,1024]{1,0:T(8,128)} %panel.1, f32[64,128]{1,0:T(8,128)} %saved.1), custom_call_target="tpu_custom_call" | custom-call | tf_op jit(solution)/shard_map/pallas_call | solution.py:385
  156.8 2.1 %copy.7 = f32[192,1024]{1,0:T(8,128)} copy(f32[192,1024]{1,0:T(8,128)} %get-tuple-element.4) | data formatting | bytes 1572864
  158.9 1.4 copy.8

commit v2 on v0

v2 whole, which is shorter than its diff:
```python
import jax
import jax.numpy as jnp
from jax import lax
from jax.experimental import pallas as pl
from jax.experimental.pallas import tpu as pltpu
from jax.sharding import PartitionSpec as P

MESH = pl.DeviceIdType.MESH
F32 = jnp.float32
BF16 = jnp.bfloat16
CHUNKS = ((0, (0,)), (1, (0, 1)), (2, (0, 1)), (3, (0, 1)), (0, (1,)))
J = len(CHUNKS)
WIDTHS = tuple(128 * len(zls) for _, zls in CHUNKS)
H = 128
R = 192
K = 3072
SLAB = 256
SLABS = K // SLAB
STAGES = tuple(j for j in range(J) if WIDTHS[j] == SLAB)[:3]

ORDER = (
    ("p0", 0), ("perm1",), ("p0", 1), ("sp", 4), ("sp", 5), ("sp", 6), ("sp", 7), ("sp", 8), ("sp", 9), ("sp", 10),
    ("sp", 11), ("p1a", 0), ("p1b", 0), ("p2", 0), ("p1a", 1), ("p1b", 1), ("p2", 1), ("p3", 0), ("p4b", 0),
    ("p4a", 0), ("p4c", 0), ("p0", 2), ("p4b", 1), ("p3", 1), ("p0", 3), ("cv", 0), ("A", 0), ("p4a", 1), ("p0", 4),
    ("BC", 0), ("p1a", 2), ("p1b", 2), ("D", 0), ("p4c", 1), ("p1b", 3), ("p2", 2), ("r1", 0), ("p1a", 3), ("p1b", 4),
    ("p1a", 4), ("cv", 1), ("A", 1), ("p3", 2), ("p2", 3), ("BC", 1), ("r2", 0), ("p4a", 2), ("p4b", 2), ("D", 1),
    ("p4c", 2), ("r1", 1), ("p4b", 3), ("p3", 4), ("p3", 3), ("p2", 4), ("cv", 2), ("r3", 0), ("perm2",), ("p4a", 3),
    ("A", 2), ("BC", 2), ("r2", 1), ("p4c", 3), ("p4a", 4), ("p4b", 4), ("p4c", 4), ("D", 2), ("r1", 2), ("cv", 3),
    ("A", 3), ("BC", 3), ("r2", 2), ("r3", 1), ("take",), ("gr", 0), ("gr", 1), ("r4", 0), ("r1", 3), ("D", 3),
    ("r3", 2), ("r4", 1), ("gr", 2), ("cv", 4), ("A", 4), ("r2", 3), ("r4", 2), ("BC", 4), ("r1", 4), ("D", 4),
    ("r3", 3), ("gr", 3), ("r5", 1), ("r2", 4), ("r5", 0), ("r4", 3), ("r3", 4), ("gr", 4), ("r5", 2), ("r4", 4),
    ("r5", 3), ("r5", 4), ("r6", 0), ("r6", 1), ("r6", 2), ("r6", 3), ("r6", 4),
)


def dot(a, b):
    return jnp.dot(a, b, preferred_element_type=F32)


def split(value):
    high = value.astype(BF16)
    return high, (value - high.astype(F32)).astype(BF16)


def kernel(*refs):
    pi, panel, out, diag, pih, pil, bh, bl, rows, mid, pth, ptl, fin = refs[:13]
    rest = refs[13:]
    gath, x1r, x2f, x2b, zrec, part, gp, gsr, a2a, fsend = (rest[i * J:(i + 1) * J] for i in range(10))
    (pisem, locsem, ag_s, ag_r, rs_s, rs_r, g_s, g_r, a_s, a_r, f_s, f_r,
     p1_s, p1_r, p2_s, p2_r) = rest[10 * J:]
    r, c = lax.axis_index("row"), lax.axis_index("col")
    zh, y, k = r // 8, (r // 2) % 4, r % 2
    zl, x = c // 4, c % 4
    z = zh * 2 + zl
    d = 1 - 2 * k

    def dev(z_, y_, x_, k_):
        return ((z_ // 2) * 8 + y_ * 2 + k_, (z_ % 2) * 4 + x_)

    def slot(zh_, y_, k_):
        return zh_ * 8 + y_ * 2 + k_

    yf, yb, y2 = (y + d + 4) % 4, (y - d + 4) % 4, (y + 2) % 4
    xf, xb, x2 = (x + d + 4) % 4, (x - d + 4) % 4, (x + 2) % 4
    zp, zt = zh * 2 + (1 - zl), (z + 2) % 4
    zo = 1 - zh
    sib = dev(z, y, x, 1 - k)
    to_yf, to_yb = dev(z, yf, x, k), dev(z, yb, x, k)
    to_zt, to_zp = dev(zt, y, x, k), dev(zp, y, x, k)
    to_xf, to_xb = dev(z, y, xf, k), dev(z, y, xb, k)

    def remote(src, dst, ss, rs, to):
        return pltpu.make_async_remote_copy(
            src_ref=src, dst_ref=dst, send_sem=ss, recv_sem=rs, device_id=to, device_id_type=MESH
        )

    def arrived(at, ss, rs):
        remote(at, at, ss, rs, sib).wait_recv()

    def sent(at, ss):
        remote(at, at, ss, p1_s, sib).wait_send()

    def columns(j, h):
        x_, zls = CHUNKS[j]
        return pl.ds((zls[h] * 4 + x_) * H, H)

    def own_copy(j, h):
        return pltpu.make_async_copy(
            panel.at[:, columns(j, h)], gath[j].at[r, :, pl.ds(h * H, H)], locsem.at[j, h]
        )

    def slab_copy(s):
        b = s % 3
        return pltpu.make_async_copy(pi.at[:, :, pl.ds(s * SLAB, SLAB)], part[STAGES[b]], pisem.at[b])

    for h in range(len(CHUNKS[0][1])):
        own_copy(0, h).start()
    for s in range(3):
        slab_copy(s).start()
    for j in range(1, J):
        for h in range(len(CHUNKS[j][1])):
            own_copy(j, h).start()

    barrier = pltpu.get_barrier_semaphore()
    peers = [to_yf, to_yb, to_zt, to_zp, sib]
    for dx in range(1, 4):
        for k_ in range(2):
            peers.append(dev(z, y, (x + dx) % 4, k_))
    for to in peers:
        pl.semaphore_signal(barrier, inc=1, device_id=to, device_id_type=MESH)

    def split_slab(s):
        b = part[STAGES[s % 3]]
        slab_copy(s).wait()

        def piece(q, carry):
            high, low = split(b[q])
            at = pl.ds(pl.multiple_of(((q % 4) * 2 + q // 4) * R, R), R)
            pih[at, s * SLAB:(s + 1) * SLAB] = high
            pil[at, s * SLAB:(s + 1) * SLAB] = low
            return carry

        lax.fori_loop(0, 8, piece, 0)
        if s + 3 < SLABS:
            slab_copy(s + 3).start()

    got = [slot(zh, yb, k), slot(zh, yf, k), slot(zo, y, k), None, slot(zo, yb, k), slot(zo, yf, k),
           slot(zh, y2, k), slot(zo, y2, k)]
    sib_slots = [slot(zh, y, k), got[0], got[1], got[2], got[6], got[4], got[5], got[7]]
    def ag(j, m):
        if m >= 8:
            source, to = sib_slots[m - 8], sib
        else:
            source = {0: r, 1: r, 2: r, 4: got[2], 5: got[2], 6: got[0], 7: got[6]}[m]
            to = {1: to_yb, 5: to_yb, 2: to_zt, 7: to_zt}.get(m, to_yf)
        at = gath[j].at[source]
        return remote(at, at, ag_s.at[j], ag_r.at[j, min(m, 8)], to)

    def ag_wait(j, m):
        at = gath[j].at[got[m]]
        arrived(at, ag_s.at[j], ag_r.at[j, m])

    def p0(j):
        for h in range(len(CHUNKS[j][1])):
            own_copy(j, h).wait()
        for m in (0, 2, 1, 8):
            ag(j, m).start()

    def relay(wait, *starts):
        def step(j):
            ag_wait(j, wait)
            for m in starts:
                ag(j, m).start()
        return step

    def cv(j):
        arrived(gath[j].at[0:8], ag_s.at[j], ag_r.at[j, 8])

        def body(q, carry):
            high, low = split(gath[j][q])
            at = pl.ds(pl.multiple_of(q * R, R), R)
            bh[at, :WIDTHS[j]] = high
            bl[at, :WIDTHS[j]] = low
            return carry

        lax.fori_loop(0, 16, body, 0)

    def compute(j, pair):
        at = pl.ds(pl.multiple_of(pair * (2 * R), 2 * R), 2 * R)
        high, low = bh[:, :WIDTHS[j]], bl[:, :WIDTHS[j]]
        total = dot(pih[at, :], high) + dot(pih[at, :], low) + dot(pil[at, :], high)
        part[j][pl.ds(pair * 2, 2)] = total.reshape(2, R, WIDTHS[j])

    def rs(j, m):
        ss, rs_ = rs_s.at[j], rs_r.at[j, m]
        if m == 0:
            return remote(part[j].at[pl.ds(x2 * 2, 2)], x1r[j], ss, rs_, to_xf)
        if m == 1:
            return remote(part[j].at[pl.ds(xb * 2, 2)], x2b[j], ss, rs_, to_xb)
        if m == 2:
            return remote(part[j].at[pl.ds(xf * 2, 2)], x2f[j], ss, rs_, to_xf)
        return remote(part[j].at[x * 2 + (1 - zl)], zrec[j], ss, rs_, to_zp)

    def qa(j):
        compute(j, x2)
        rs(j, 0).start()

    def qbc(j):
        def body(i, carry):
            compute(j, jnp.where(i == 0, xb, xf))

            @pl.when(i == 0)
            def _():
                rs(j, 1).start()

            return carry

        lax.fori_loop(0, 2, body, 0)

    def qd(j):
        compute(j, x)

    def r1(j):
        rs(j, 0).wait_recv()
        at = pl.ds(xf * 2, 2)
        part[j][at] = part[j][at] + x1r[j][...]
        rs(j, 2).start()

    def r2(j):
        rs(j, 1).wait_recv()
        rs(j, 2).wait_recv()
        q = 1 - zl
        part[j][x * 2 + q] = part[j][x * 2 + q] + x2f[j][q] + x2b[j][q]
        rs(j, 3).start()
        part[j][x * 2 + zl] = part[j][x * 2 + zl] + x2f[j][zl] + x2b[j][zl]

    def r3(j):
        rs(j, 3).wait_recv()
        product = part[j][x * 2 + zl] + zrec[j][...]
        part[j][x * 2 + zl] = product
        for h in range(len(CHUNKS[j][1])):
            out[:, columns(j, h)] = product[:, h * H:(h + 1) * H]

    def sib_gram(j):
        return remote(gp[j].at[:, 1 - k], gsr[j], g_s.at[j], g_r.at[j], sib)

    def gr(j):
        high, low = split(part[j][x * 2 + zl])
        for i in range(8):
            at = pl.ds(i * H, H)
            tile = dot(pth[at, :], high) + dot(pth[at, :], low) + dot(ptl[at, :], high)
            gp[j][i] = tile.reshape(2, 64, WIDTHS[j])
        sib_gram(j).start()

    def gram_to(j, i):
        zls = CHUNKS[j][1]
        if len(zls) == 2:
            z_ = (z + i // 4) % 4
            at = z_ % 2
        else:
            z_ = ((zh + i // 4) % 2) * 2 + zls[0]
            at = 0
        y_ = (y + i % 4) % 4
        source = gp[j].at[(z_ // 2) * 4 + y_, k, :, pl.ds(pl.multiple_of(at * H, H), H)]
        s = ((z_ - z + 4) % 4) * 4 + i % 4
        return remote(source, a2a[j].at[s], a_s.at[j], a_r.at[j], dev(z_, y_, x, k))

    def r4(j):
        arrived(gsr[j], g_s.at[j], g_r.at[j])
        for i in range(8):
            gp[j][i, k] = gp[j][i, k] + gsr[j][i]
        both = len(CHUNKS[j][1]) == 2
        for i in range(8 * len(CHUNKS[j][1])):
            if i or not both:
                copy = gram_to(j, i)
                copy.start() if i else pl.when(zl != CHUNKS[j][1][0])(copy.start)

    def takes(j, act):
        zls = CHUNKS[j][1]
        if len(zls) == 2:
            act()
        else:
            pl.when(zl == zls[0])(act)

    def last(j):
        x_ = CHUNKS[j][0]
        dx = (x - x_ + 4) % 4
        return remote(fsend[j], fin.at[dx], f_s.at[j], f_r.at[dx], dev(z, y, x_, k))

    def r5(j):
        def act():
            at = zl * H if len(CHUNKS[j][1]) == 2 else 0
            own = gp[j][zh * 4 + y, k, :, pl.ds(pl.multiple_of(at, H), H)]

            arrived(a2a[j].at[1:16], a_s.at[j], a_r.at[j])
            parts = [own] + [a2a[j][i] for i in range(1, 16)]
            while len(parts) > 1:
                parts = [a + b for a, b in zip(parts[::2], parts[1::2])]
            fsend[j][...] = parts[0]

            @pl.when(x != CHUNKS[j][0])
            def _():
                last(j).start()

        takes(j, act)

    def r6(j):
        def act():
            @pl.when(x == CHUNKS[j][0])
            def _():
                total = fsend[j][...]
                for dx in range(1, 4):
                    arrived(fin.at[dx], f_s.at[j], f_r.at[dx])
                    total = total + fin[dx]
                diag[...] = total

        takes(j, act)

    to_mid = dev(z, y, 2 * (y % 2) + k, x % 2)
    stays = jnp.logical_and(x == 2 * (y % 2) + k, x % 2 == k)
    is_mid = x // 2 == y % 2
    lands = jnp.logical_and(
        jnp.logical_and(y % 2 == k, zl == zh),
        jnp.logical_and(jnp.logical_and(y // 2 == zl, zh == k), is_mid),
    )
    perm1_copy = remote(panel, mid.at[x // 2], p1_s, p1_r.at[x // 2], to_mid)
    perm1_self = pltpu.make_async_copy(panel, mid.at[x // 2], p1_r.at[x // 2])

    def perm1():
        @pl.when(stays)
        def _():
            perm1_self.start()

        @pl.when(jnp.logical_not(stays))
        def _():
            perm1_copy.start()

    def perm2_copy(m):
        return remote(mid.at[m], rows, p2_s.at[m], p2_r, dev(2 * zl + y // 2, 2 * m + k, x, zh))

    def perm2_self(m):
        return pltpu.make_async_copy(mid.at[m], rows, p2_r)

    def perm2():
        @pl.when(is_mid)
        def _():
            for m in range(2):
                here = jnp.logical_and(stays, x // 2 == m)

                @pl.when(here)
                def _():
                    pltpu.make_async_copy(panel, mid.at[m], p1_r.at[m]).wait()

                @pl.when(jnp.logical_not(here))
                def _():
                    arrived(mid.at[m], p1_s, p1_r.at[m])

            for m in range(2):
                here = jnp.logical_and(lands, y // 2 == m)

                @pl.when(here)
                def _():
                    perm2_self(m).start()

                @pl.when(jnp.logical_not(here))
                def _():
                    perm2_copy(m).start()

    def take():
        @pl.when(lands)
        def _():
            perm2_self(0).wait()

        @pl.when(jnp.logical_not(lands))
        def _():
            arrived(rows, p2_s.at[0], p2_r)

        for i in range(8):
            high, low = split(rows[:, i * H:(i + 1) * H].T)
            pth[i * H:(i + 1) * H, :] = high
            ptl[i * H:(i + 1) * H, :] = low

    for s in range(4):
        split_slab(s)
    pl.semaphore_wait(barrier, len(peers))

    steps = {
        "sp": split_slab, "p0": p0, "p1a": relay(0, 6, 9), "p1b": relay(1, 10), "p2": relay(2, 4, 5, 11),
        "p3": relay(6, 7, 12), "p4a": relay(4, 13), "p4b": relay(5, 14), "p4c": relay(7, 15),
        "cv": cv, "A": qa, "BC": qbc, "D": qd, "r1": r1, "r2": r2, "r3": r3, "gr": gr,
        "r4": r4, "r5": r5, "r6": r6, "perm1": perm1, "perm2": perm2, "take": take,
    }
    for step in ORDER:
        steps[step[0]](*step[1:])

    for j in range(J):
        sent(gath[j].at[0:15], ag_s.at[j])
        sent(gath[j].at[0:7], rs_s.at[j])
        sib_gram(j).wait_send()
        if len(CHUNKS[j][1]) == 2:
            sent(a2a[j].at[0:15], a_s.at[j])
        else:
            @pl.when(zl == CHUNKS[j][1][0])
            def _():
                sent(a2a[j].at[0:7], a_s.at[j])

            @pl.when(zl != CHUNKS[j][1][0])
            def _():
                sent(a2a[j].at[0:8], a_s.at[j])

        def final(j=j):
            @pl.when(x != CHUNKS[j][0])
            def _():
                last(j).wait_send()

        takes(j, final)

    @pl.when(jnp.logical_not(stays))
    def _():
        perm1_copy.wait_send()

    @pl.when(is_mid)
    def _():
        for m in range(2):
            @pl.when(jnp.logical_not(jnp.logical_and(lands, y // 2 == m)))
            def _():
                perm2_copy(m).wait_send()


def shards(parent_inverse, panel, saved_diag):
    vmem = pl.BlockSpec(memory_space=pltpu.VMEM)
    hbm = pl.BlockSpec(memory_space=pl.ANY)
    dma = pltpu.SemaphoreType.DMA

    def each(*shape):
        return [pltpu.VMEM(shape + (w,), F32) for w in WIDTHS]

    product, gram = pl.pallas_call(
        kernel,
        out_shape=(
            jax.ShapeDtypeStruct((R, 1024), F32),
            jax.ShapeDtypeStruct((64, H), F32),
        ),
        in_specs=[hbm, hbm],
        out_specs=(vmem, vmem),
        scratch_shapes=[
            pltpu.VMEM((8 * R, K), BF16),
            pltpu.VMEM((8 * R, K), BF16),
            pltpu.VMEM((K, max(WIDTHS)), BF16),
            pltpu.VMEM((K, max(WIDTHS)), BF16),
            pltpu.VMEM((R, 1024), F32),
            pltpu.VMEM((2, R, 1024), F32),
            pltpu.VMEM((1024, R), BF16),
            pltpu.VMEM((1024, R), BF16),
            pltpu.VMEM((4, 64, H), F32),
            *each(16, R),
            *each(2, R),
            *each(2, R),
            *each(2, R),
            *each(R),
            *each(8, R),
            *each(8, 2, 64),
            *each(8, 64),
            *[pltpu.VMEM((16, 64, H), F32) for _ in range(J)],
            *[pltpu.VMEM((64, H), F32) for _ in range(J)],
            dma((3,)),
            dma((J, 2)),
            dma((J,)),
            dma((J, 9)),
            dma((J,)),
            dma((J, 4)),
            dma((J,)),
            dma((J,)),
            dma((J,)),
            dma((J,)),
            dma((J,)),
            dma((4,)),
            dma,
            dma((2,)),
            dma((2,)),
            dma,
        ],
        compiler_params=pltpu.CompilerParams(
            collective_id=0, has_side_effects=True, vmem_limit_bytes=67043328
        ),
    )(parent_inverse.reshape(8, R, K), panel)
    return -product, saved_diag + gram


def solution(mesh):
    in_specs = (P("row", "col"), P(("col", "row"), None), P("row", "col"))
    out_specs = (P(("row", "col"), None), P("row", "col"))
    return jax.shard_map(shards, mesh=mesh, in_specs=in_specs, out_specs=out_specs, check_vma=False)
```

time: 462 us -> 135 us (0.29)
  waiting for transfers between devices: 363 us -> 0 us
  Pallas kernels: 0 us -> 130 us
  matrix products: 73.8 us -> 0 us
  between operations: 13.8 us -> 0.64 us
  other arithmetic: 9.07 us -> 3.49 us
    reduce_scatter x3 -> x0, waiting for transfers between devices: 194 us -> none  [the longest x1 74.2 us: shards(): lax.psum_scatter(jnp.dot(parent_inverse, column_panel, precision=lax.Prec...]
    pallas_call x0 -> x1, Pallas kernels: none -> 130 us  [shards(): pl.pallas_call(kernel, out_shape=(jax.ShapeDtypeStruct((R, 1024), F32), j...]
    all_gather x1 -> x0, waiting for transfers between devices: 92.4 us -> none  [shards(): column_panel = lax.all_gather(panel, 'row', axis=0, tiled=True)]
    psum x1 -> x0, waiting for transfers between devices: 76.3 us -> none  [spread(): return lax.psum(block, axis)]
    dot_general x2 -> x0, matrix products: 73.8 us -> none  [the longest x1 66.9 us: shards(): jnp.dot(parent_inverse, column_panel, precision=lax.Precision.HIGHEST, pr...]
    select_n x1 -> x0, other arithmetic: 6.75 us -> none  [spread(): jnp.where(lax.axis_index(axis) == holder, block, jnp.zeros_like(block))]
  transfers between devices with their start and end apart: 5 -> 0, of which waited for: 5 -> 0; matrix products, arithmetic and copies ran while one was open for 15% -> 0% of each run, Pallas kernels for 0% -> 0%
where the time goes in v2:
time: 135 us; the launch traced here: 134 us
  Pallas kernels  130 us (96%)
  other arithmetic  3.49 us (3%)
    pallas_call x1, Pallas kernels, shards(): pl.pallas_call(kernel, out_shape=(jax.ShapeDtypeStruct((R, 1024), F32), j...  130 us

profile of v2, /device:TPU:96, one launch (start us, length us, event | category | flops | bytes accessed | tf_op | source)
XLA Modules:
  0.0 134.3 jit_solution(13907161693386503650)
XLA Ops:
  0.6 130.2 %shard_map.50 = (f32[192,1024]{1,0:T(8,128)}, f32[64,128]{1,0:T(8,128)}) custom-call(f32[8,192,3072]{2,1,0:T(8,128)} %bitcast.1, f32[192,1024]{1,0:T(8,128)} %refs_1_.1), custom_call_target="tpu_custom_call" | custom-call | tf_op jit(solution)/shard_map/pallas_call | solution.py:418
  130.8 2.1 %neg.3 = f32[192,1024]{1,0:T(8,128)} negate(f32[192,1024]{1,0:T(8,128)} %get-tuple-element.4) | non-fusion elementwise | flops 196608 | bytes 1572864 | tf_op jit(solution)/shard_map/neg | solution.py:467
  132.9 1.4 %add.3 = f32[64,128]{1,0:T(8,128)} add(f32[64,128]{1,0:T(8,128)} %param.5, f32[64,128]{1,0:T(8,128)} %get-tuple-element.5) | non-fusion elementwise | flops 8192 | bytes 98304 | tf_op jit(solution)/shard_map/add | solution.py:467

commit v3 on v2

--- a/solution.py
+++ b/solution.py
@@ -17,6 +17,8 @@
 SLAB = 256
 SLABS = K // SLAB
 STAGES = tuple(j for j in range(J) if WIDTHS[j] == SLAB)[:3]
+
+ACROSS = ()
 
 ORDER = (
     ("p0", 0), ("perm1",), ("p0", 1), ("sp", 4), ("sp", 5), ("sp", 6), ("sp", 7), ("sp", 8), ("sp", 9), ("sp", 10),
@@ -159,22 +161,33 @@
         def body(q, carry):
             high, low = split(gath[j][q])
             at = pl.ds(pl.multiple_of(q * R, R), R)
-            bh[at, :WIDTHS[j]] = high
-            bl[at, :WIDTHS[j]] = low
+            if WIDTHS[j] == H:
+                bh[at, :H] = high
+                bh[at, H:] = low
+            else:
+                bh[at, :] = high
+                bl[at, :] = low
             return carry
 
         lax.fori_loop(0, 16, body, 0)
 
     def compute(j, pair):
         at = pl.ds(pl.multiple_of(pair * (2 * R), 2 * R), 2 * R)
-        high, low = bh[:, :WIDTHS[j]], bl[:, :WIDTHS[j]]
-        total = dot(pih[at, :], high) + dot(pih[at, :], low) + dot(pil[at, :], high)
+        if WIDTHS[j] == H:
+            wide = dot(pih[at, :], bh[...])
+            total = wide[:, :H] + wide[:, H:] + dot(pil[at, :], bh[:, :H])
+        else:
+            total = dot(pih[at, :], bh[...]) + dot(pih[at, :], bl[...]) + dot(pil[at, :], bh[...])
         part[j][pl.ds(pair * 2, 2)] = total.reshape(2, R, WIDTHS[j])
 
     def rs(j, m):
         ss, rs_ = rs_s.at[j], rs_r.at[j, m]
+        if m == 0 and j in ACROSS:
+            return remote(part[j].at[x2 * 2 + zl], x1r[j].at[0], ss, rs_, to_xf)
         if m == 0:
             return remote(part[j].at[pl.ds(x2 * 2, 2)], x1r[j], ss, rs_, to_xf)
+        if m == 4:
+            return remote(part[j].at[x2 * 2 + (1 - zl)], x1r[j].at[1], ss, rs_, to_zp)
         if m == 1:
             return remote(part[j].at[pl.ds(xb * 2, 2)], x2b[j], ss, rs_, to_xb)
         if m == 2:
@@ -183,6 +196,11 @@
 
     def qa(j):
         compute(j, x2)
+        rs(j, 4 if j in ACROSS else 0).start()
+
+    def r0(j):
+        rs(j, 4).wait_recv()
+        part[j][x2 * 2 + zl] = part[j][x2 * 2 + zl] + x1r[j][1]
         rs(j, 0).start()
 
     def qbc(j):
@@ -202,8 +220,11 @@
 
     def r1(j):
         rs(j, 0).wait_recv()
-        at = pl.ds(xf * 2, 2)
-        part[j][at] = part[j][at] + x1r[j][...]
+        if j in ACROSS:
+            part[j][xf * 2 + zl] = part[j][xf * 2 + zl] + x1r[j][0]
+        else:
+            at = pl.ds(xf * 2, 2)
+            part[j][at] = part[j][at] + x1r[j][...]
         rs(j, 2).start()
 
     def r2(j):
@@ -367,7 +388,7 @@
     steps = {
         "sp": split_slab, "p0": p0, "p1a": relay(0, 6, 9), "p1b": relay(1, 10), "p2": relay(2, 4, 5, 11),
         "p3": relay(6, 7, 12), "p4a": relay(4, 13), "p4b": relay(5, 14), "p4c": relay(7, 15),
-        "cv": cv, "A": qa, "BC": qbc, "D": qd, "r1": r1, "r2": r2, "r3": r3, "gr": gr,
+        "cv": cv, "A": qa, "BC": qbc, "D": qd, "r0": r0, "r1": r1, "r2": r2, "r3": r3, "gr": gr,
         "r4": r4, "r5": r5, "r6": r6, "perm1": perm1, "perm2": perm2, "take": take,
     }
     for step in ORDER:
@@ -448,7 +469,7 @@
             dma((J,)),
             dma((J, 9)),
             dma((J,)),
-            dma((J, 4)),
+            dma((J, 5)),
             dma((J,)),
             dma((J,)),
             dma((J,)),

time: 135 us -> 131 us (0.970)
  Pallas kernels: 130 us -> 126 us
    pallas_call x1, Pallas kernels: 130 us -> 126 us  [shards(): pl.pallas_call(kernel, out_shape=(jax.ShapeDtypeStruct((R, 1024), F32), j...]
where the time goes in v3:
time: 131 us; the launch traced here: 130 us
  Pallas kernels  126 us (96%)
  other arithmetic  3.49 us (3%)
    pallas_call x1, Pallas kernels, shards(): pl.pallas_call(kernel, out_shape=(jax.ShapeDtypeStruct((R, 1024), F32), j...  126 us

profile of v3, /device:TPU:96, one launch (start us, length us, event | category | flops | bytes accessed | tf_op | source)
XLA Modules:
  0.0 130.1 jit_solution(5377515450493380334)
XLA Ops:
  0.6 125.9 %shard_map.50 = (f32[192,1024]{1,0:T(8,128)}, f32[64,128]{1,0:T(8,128)}) custom-call(f32[8,192,3072]{2,1,0:T(8,128)} %bitcast.1, f32[192,1024]{1,0:T(8,128)} %refs_1_.1), custom_call_target="tpu_custom_call" | custom-call | tf_op jit(solution)/shard_map/pallas_call | solution.py:439
  126.6 2.1 %neg.3 = f32[192,1024]{1,0:T(8,128)} negate(f32[192,1024]{1,0:T(8,128)} %get-tuple-element.4) | non-fusion elementwise | flops 196608 | bytes 1572864 | tf_op jit(solution)/shard_map/neg | solution.py:488
  128.7 1.4 %add.3 = f32[64,128]{1,0:T(8,128)} add(f32[64,128]{1,0:T(8,128)} %param.5, f32[64,128]{1,0:T(8,128)} %get-tuple-element.5) | non-fusion elementwise | flops 8192 | bytes 98304 | tf_op jit(solution)/shard_map/add | solution.py:488

commit v4 on v3

--- a/solution.py
+++ b/solution.py
@@ -21,17 +21,17 @@
 ACROSS = ()
 
 ORDER = (
-    ("p0", 0), ("perm1",), ("p0", 1), ("sp", 4), ("sp", 5), ("sp", 6), ("sp", 7), ("sp", 8), ("sp", 9), ("sp", 10),
-    ("sp", 11), ("p1a", 0), ("p1b", 0), ("p2", 0), ("p1a", 1), ("p1b", 1), ("p2", 1), ("p3", 0), ("p4b", 0),
-    ("p4a", 0), ("p4c", 0), ("p0", 2), ("p4b", 1), ("p3", 1), ("p0", 3), ("cv", 0), ("A", 0), ("p4a", 1), ("p0", 4),
-    ("BC", 0), ("p1a", 2), ("p1b", 2), ("D", 0), ("p4c", 1), ("p1b", 3), ("p2", 2), ("r1", 0), ("p1a", 3), ("p1b", 4),
-    ("p1a", 4), ("cv", 1), ("A", 1), ("p3", 2), ("p2", 3), ("BC", 1), ("r2", 0), ("p4a", 2), ("p4b", 2), ("D", 1),
-    ("p4c", 2), ("r1", 1), ("p4b", 3), ("p3", 4), ("p3", 3), ("p2", 4), ("cv", 2), ("r3", 0), ("perm2",), ("p4a", 3),
-    ("A", 2), ("BC", 2), ("r2", 1), ("p4c", 3), ("p4a", 4), ("p4b", 4), ("p4c", 4), ("D", 2), ("r1", 2), ("cv", 3),
-    ("A", 3), ("BC", 3), ("r2", 2), ("r3", 1), ("take",), ("gr", 0), ("gr", 1), ("r4", 0), ("r1", 3), ("D", 3),
-    ("r3", 2), ("r4", 1), ("gr", 2), ("cv", 4), ("A", 4), ("r2", 3), ("r4", 2), ("BC", 4), ("r1", 4), ("D", 4),
-    ("r3", 3), ("gr", 3), ("r5", 1), ("r2", 4), ("r5", 0), ("r4", 3), ("r3", 4), ("gr", 4), ("r5", 2), ("r4", 4),
-    ("r5", 3), ("r5", 4), ("r6", 0), ("r6", 1), ("r6", 2), ("r6", 3), ("r6", 4),
+    ("p0", 0), ("p0", 1), ("perm1",), ("p1a", 0), ("p2", 0), ("p1a", 1), ("sp", 4), ("sp", 5), ("p3", 0), ("p1b", 1),
+    ("sp", 6), ("sp", 7), ("p2", 1), ("p1b", 0), ("sp", 8), ("sp", 9), ("p3", 1), ("p0", 2), ("sp", 10), ("sp", 11),
+    ("p4b", 0), ("p4a", 0), ("p4c", 0), ("p0", 3), ("cv", 0), ("A", 0), ("BC", 0), ("p1a", 2), ("p4c", 1), ("p1b", 2),
+    ("p4a", 1), ("p4b", 1), ("D", 0), ("r1", 0), ("cv", 1), ("p2", 2), ("p0", 4), ("A", 1), ("p1a", 3), ("p3", 2),
+    ("p2", 3), ("r2", 0), ("BC", 1), ("p1b", 4), ("D", 1), ("p4c", 2), ("p1a", 4), ("p1b", 3), ("p4b", 2), ("p4a", 2),
+    ("r3", 0), ("r1", 1), ("p3", 3), ("perm2",), ("cv", 2), ("A", 2), ("p2", 4), ("BC", 2), ("p4a", 3), ("p4c", 3),
+    ("r2", 1), ("p4b", 3), ("p3", 4), ("D", 2), ("cv", 3), ("r1", 2), ("A", 3), ("BC", 3), ("r3", 1), ("r2", 2),
+    ("take",), ("gr", 0), ("gr", 1), ("p4c", 4), ("r4", 0), ("r1", 3), ("p4a", 4), ("p4b", 4), ("r4", 1), ("D", 3),
+    ("cv", 4), ("r3", 2), ("gr", 2), ("A", 4), ("r2", 3), ("r4", 2), ("BC", 4), ("r1", 4), ("D", 4), ("r5", 1),
+    ("r3", 3), ("gr", 3), ("r2", 4), ("r4", 3), ("r6", 1), ("r5", 0), ("r3", 4), ("gr", 4), ("r5", 2), ("r4", 4),
+    ("r5", 3), ("r5", 4), ("r6", 2), ("r6", 3), ("r6", 4), ("r6", 0),
 )
 
 

time: 131 us -> 125 us (0.954)
  Pallas kernels: 126 us -> 121 us
    pallas_call x1, Pallas kernels: 126 us -> 121 us  [shards(): pl.pallas_call(kernel, out_shape=(jax.ShapeDtypeStruct((R, 1024), F32), j...]
where the time goes in v4:
time: 125 us
  Pallas kernels  121 us (97%)
  other arithmetic  3.49 us (3%)
    pallas_call x1, Pallas kernels, shards(): pl.pallas_call(kernel, out_shape=(jax.ShapeDtypeStruct((R, 1024), F32), j...  121 us

profile of v4, /device:TPU:96, one launch (start us, length us, event | category | flops | bytes accessed | tf_op | source)
XLA Modules:
  0.0 125.0 jit_solution(17819382093045053026)
XLA Ops:
  0.6 120.9 %shard_map.50 = (f32[192,1024]{1,0:T(8,128)}, f32[64,128]{1,0:T(8,128)}) custom-call(f32[8,192,3072]{2,1,0:T(8,128)} %bitcast.1, f32[192,1024]{1,0:T(8,128)} %refs_1_.1), custom_call_target="tpu_custom_call" | custom-call | tf_op jit(solution)/shard_map/pallas_call | solution.py:439
  121.5 2.1 %neg.3 = f32[192,1024]{1,0:T(8,128)} negate(f32[192,1024]{1,0:T(8,128)} %get-tuple-element.4) | non-fusion elementwise | flops 196608 | bytes 1572864 | tf_op jit(solution)/shard_map/neg | solution.py:488
  123.6 1.4 %add.3 = f32[64,128]{1,0:T(8,128)} add(f32[64,128]{1,0:T(8,128)} %param.5, f32[64,128]{1,0:T(8,128)} %get-tuple-element.5) | non-fusion elementwise | flops 8192 | bytes 98304 | tf_op jit(solution)/shard_map/add | solution.py:488
